TPU v7x, 256 devices: a whole 4x4x8 slice. The times are simulated.
256 devices in a mesh: tm: 32 (over y_lo, z, core), gy: 8 (over y_hi, x).
Axes of the slice: x: 4, y: 4 (y_hi: 2, y_lo: 2; y = y_hi * 2 + y_lo), z: 8, core: 2. Of those that a mesh axis runs over, the one named last changes fastest.
Arguments:
- magnetic: bfloat16 [32, 3, 3, 1024, 1024], P('tm', None, None, 'gy'), may hold values from -6 to 6
- velocity: bfloat16 [32, 3, 1, 1024, 1024], P('tm', None, None, 'gy'), may hold values from -6 to 6
- mode_bin: int32 [1024, 1024], P(None, 'gy'), may hold values from 0 to 127, as said below
- omega_edges: int32 [9], replicated, may hold values from 0 to 32, as said below
Outputs:
- power: float32 [32, 1024, 1024], P('tm', None, 'gy')
- spectrum: float32 [8, 128], replicated
Inputs may be any that keep to these rules, and one draw needn't show every extreme that they name: mode_bin = 16 * p + q, where p is a level of min(kz, 1024 - kz) and q a level of min(ky, 1024 - ky); levels never fall as the wavenumber rises, and every value occurs. `omega_edges`: edges rise strictly, the first 0 and the last 32.
All inputs are finite; a program needn't handle non-finite values.
Results may differ from a plain program's by a relative error of at most 0.004.
The roundings to bfloat16 on the way count: a program that leaves them out, or rounds other values in their place, can miss the bound.
Values may be sent and summed in bfloat16 or wider, within the bound.
No kernel may reach another device: no remote copies, remote signals or barrier semaphores. Data moves between devices by JAX's collectives and lax.ppermute only.
A program may use at most 128 MiB of HBM per device.

v0:
```python
import math
import jax
import jax.numpy as jnp
from jax import lax
from jax.sharding import PartitionSpec as P

NBP = 8
NBQ = 16
NB_W = 8
hall_coef = 1.0
highest = lax.Precision.HIGHEST


def extended(cells, sides, width):
    for axis, dim in sides:
        count = lax.axis_size(axis)
        head = lax.slice_in_dim(cells, 0, width, axis=dim)
        tail = lax.slice_in_dim(cells, cells.shape[dim] - width, cells.shape[dim], axis=dim)
        cells = jnp.concatenate(
            [
                lax.ppermute(tail, axis, [(i, (i + 1) % count) for i in range(count)]),
                cells,
                lax.ppermute(head, axis, [((i + 1) % count, i) for i in range(count)]),
            ],
            axis=dim,
        )
    return cells


def window_taper_for(sample_moments, every_time_sample):
    return 0.5 - 0.5 * jnp.cos(
        2.0 * math.pi * (sample_moments.astype(jnp.float32) + 0.5) / every_time_sample
    )


def temporal_coefficients(angular_frequency, sample_moments, every_time_sample):
    phase_angles = jnp.mod(
        angular_frequency[:, None] * sample_moments[None, :], every_time_sample
    ).astype(jnp.float32)
    angles = 2.0 * math.pi * phase_angles / every_time_sample
    taper_weight = window_taper_for(sample_moments, every_time_sample)[None, :]
    return (
        (taper_weight * jnp.cos(angles)).astype(jnp.bfloat16),
        (-taper_weight * jnp.sin(angles)).astype(jnp.bfloat16),
    )


def dft_tables(length):
    series = jnp.arange(length, dtype=jnp.int32)
    phase_angles = jnp.mod(series[:, None] * series[None, :], length).astype(jnp.float32)
    angles = 2.0 * math.pi * phase_angles / length
    return (jnp.cos(angles).astype(jnp.bfloat16), jnp.sin(angles).astype(jnp.bfloat16))


def z_slope(values):
    return (jnp.roll(values, -1, axis=-1) - jnp.roll(values, 1, axis=-1)) * 0.5


def z_turn(re_part, im_part):
    zcos_tab, zsin_tab = dft_tables(re_part.shape[-1])
    turned_re = jnp.dot(re_part, zcos_tab, preferred_element_type=jnp.float32) + jnp.dot(
        im_part, zsin_tab, preferred_element_type=jnp.float32
    )
    turned_im = jnp.dot(im_part, zcos_tab, preferred_element_type=jnp.float32) - jnp.dot(
        re_part, zsin_tab, preferred_element_type=jnp.float32
    )
    return jnp.stack([turned_re, turned_im]).astype(jnp.bfloat16)


def electric_of(magnetic, velocity, slope_magz, slope_magx):
    inner = magnetic[:, :, 1:-1].astype(jnp.float32)
    x_slope = (
        magnetic[:, :, 2:].astype(jnp.float32) - magnetic[:, :, :-2].astype(jnp.float32)
    ) * 0.5
    mag_x, mag_y, mag_z = (inner[:, 0], inner[:, 1], inner[:, 2])
    cur_x = slope_magz - z_slope(mag_y)
    cur_y = z_slope(mag_x) - x_slope[:, 2]
    cur_z = x_slope[:, 1] - slope_magx
    flow = velocity.astype(jnp.float32)
    vel_x, vel_y, vel_z = (flow[:, 0], flow[:, 1], flow[:, 2])
    elec_x = -(vel_y * mag_z - vel_z * mag_y) + hall_coef * (cur_y * mag_z - cur_z * mag_y)
    elec_y = -(vel_z * mag_x - vel_x * mag_z) + hall_coef * (cur_z * mag_x - cur_x * mag_z)
    elec_z = -(vel_x * mag_y - vel_y * mag_x) + hall_coef * (cur_x * mag_y - cur_y * mag_x)
    return jnp.stack([elec_x, elec_y, elec_z], axis=1)


def body(magnetic, velocity, mode_bin, omega_edges):
    face_rows = jnp.stack([magnetic[:, 2, 1:-1], magnetic[:, 0, 1:-1]], axis=1)
    padded = extended(face_rows, (("gy", 3),), 1)
    slopes = (
        padded[:, :, :, 2:].astype(jnp.float32) - padded[:, :, :, :-2].astype(jnp.float32)
    ) * 0.5
    electric = electric_of(magnetic, velocity, slopes[:, 0], slopes[:, 1]).astype(jnp.bfloat16)
    local_t = electric.shape[0]
    z_count = electric.shape[-1]
    every_time_sample = local_t * lax.axis_size("tm")
    half_count = every_time_sample // 2
    owner_rank = lax.axis_index("tm")
    angular_frequency = owner_rank * local_t + jnp.arange(local_t, dtype=jnp.int32) - half_count
    time_segment = lax.all_gather(electric, "tm", axis=0, tiled=True)
    sample_moments = jnp.arange(time_segment.shape[0], dtype=jnp.int32)
    coefficient_real, coefficient_imaginary = temporal_coefficients(
        angular_frequency, sample_moments, every_time_sample
    )
    re_part = jnp.einsum(
        "wt,tcxyz->wcxyz", coefficient_real, time_segment, preferred_element_type=jnp.float32
    )
    im_part = jnp.einsum(
        "wt,tcxyz->wcxyz", coefficient_imaginary, time_segment, preferred_element_type=jnp.float32
    )
    moved = lax.all_to_all(
        z_turn(re_part.astype(jnp.bfloat16), im_part.astype(jnp.bfloat16)),
        "gy",
        split_axis=5,
        concat_axis=4,
        tiled=True,
    )
    y_count = moved.shape[4]
    ycos_tab, ysin_tab = dft_tables(y_count)
    wave_re = jnp.einsum(
        "wcxyk,yq->wcxqk", moved[0], ycos_tab, preferred_element_type=jnp.float32
    ) + jnp.einsum("wcxyk,yq->wcxqk", moved[1], ysin_tab, preferred_element_type=jnp.float32)
    wave_im = jnp.einsum(
        "wcxyk,yq->wcxqk", moved[1], ycos_tab, preferred_element_type=jnp.float32
    ) - jnp.einsum("wcxyk,yq->wcxqk", moved[0], ysin_tab, preferred_element_type=jnp.float32)
    power_map = jnp.sum(wave_re * wave_re + wave_im * wave_im, axis=(1, 2)) / (
        every_time_sample * y_count * z_count
    )
    kz_local = power_map.shape[2]
    block_rows = min(64, y_count)
    bin_total = NBP * NBQ
    bin_range = jnp.arange(bin_total, dtype=jnp.int32)

    def add_block(step_num, summed):
        row_block = lax.dynamic_slice_in_dim(
            power_map, step_num * block_rows, block_rows, 1
        ).reshape(local_t, block_rows * kz_local)
        bin_ids = lax.dynamic_slice_in_dim(mode_bin, step_num * block_rows, block_rows, 0).reshape(
            block_rows * kz_local
        )
        onehot = (bin_ids[:, None] == bin_range[None, :]).astype(jnp.float32)
        return summed + jnp.dot(row_block, onehot, precision=highest)

    by_mode = lax.fori_loop(
        0, y_count // block_rows, add_block, jnp.zeros((local_t, bin_total), jnp.float32)
    )
    omega = owner_rank * local_t + jnp.arange(local_t, dtype=jnp.int32)
    member = (
        (omega[None, :] >= omega_edges[:-1, None]) & (omega[None, :] < omega_edges[1:, None])
    ).astype(jnp.float32)
    partial_value = jnp.dot(member, by_mode, precision=highest)
    binned = lax.psum(partial_value, ("tm", "gy"))
    spectrum = jnp.log(
        binned * (NB_W * bin_total) / (every_time_sample * y_count * z_count) + 1e-06
    )
    return (power_map, spectrum)


def solution(mesh):
    return jax.shard_map(
        body,
        mesh=mesh,
        in_specs=(
            P("tm", None, None, "gy", None),
            P("tm", None, None, "gy", None),
            P(None, "gy"),
            P(),
        ),
        out_specs=(P("tm", None, "gy"), P()),
        check_vma=False,
    )
```

profile of v0, /device:TPU:1, one launch (start us, length us, event | category | flops | bytes accessed | tf_op | source)
XLA Modules:
  0.0 512.5 jit_solution(18000967554781323091)
XLA Ops:
  7.2 1.2 fusion.103
  8.5 6.0 %collective-permute-start = (bf16[1,2,1,1,1024]{4,3,2,1,0:T(2,128)(2,1)S(1)}, bf16[1,2,1,1,1024]{4,3,2,1,0:T(2,128)(2,1)S(1)}, u32[]{:S(2)}, u32[]{:S(2)}) collective-permute-start(bf16[1,2,1,1,1024]{4,3,2,1,0:T(2,128)(2,1)S(1)} %get-tuple-element.139), channel_id=1, source_target_pairs={{1,0},{2,1},{3,2},{4,3},{5,4},{6,5},{7,6},{0,7},{9,8},{10,9},{11,1... | collective-permute-start | bytes 12296 | tf_op jit(solution)/shard_map/ppermute | solution.py:23
  14.5 1.4 slice_convert_fusion
  15.9 0.3 subtract_multiply_fusion
  16.2 0.2 slice_bitcast_fusion.1
  16.5 0.2 convert_element_type.197
  16.7 3.9 collective-permute-done.1
  20.6 0.3 subtract_multiply_fusion.1
  20.9 0.6 add_convert_fusion.2
  21.5 0.2 slice_bitcast_fusion.3
  21.7 0.6 add_convert_fusion.3
  22.3 0.3 add_convert_fusion.1
  22.6 1.1 pad_maximum_fusion.1
  23.7 142.3 %all-gather.2.cloned.1.call-done = bf16[32,3,1,128,1024]{4,3,2,1,0:T(8,128)(2,1)} async-done(((bf16[1,3,1,128,1024]{4,3,2,1,0:T(8,128)(2,1)}), bf16[32,3,1,128,1024]{4,3,2,1,0:T(8,128)(2,1)}) %all-gather.2.cloned.1.call-update) | async-done | bytes 25165840 | tf_op jit(solution)/shard_map/all_gather | solution.py:100
  166.0 24.4 %fusion.5 = bf16[1,3,128,1024]{3,0,2,1:T(2,128)(2,1)S(1)} fusion(bf16[32,3,128,1024]{3,2,1,0:T(8,128)(2,1)} %bitcast.97, s32[]{:T(128)S(6)} %sub.139), kind=kOutput, calls=%fused_computation.8 | convolution fusion | flops 25166528 | bytes 25952260 | tf_op jit(solution)/shard_map/wt,tcxyz->wcxyz/dot_general | solution.py:108
  190.5 24.9 %fusion.7 = bf16[1,3,128,1024]{3,0,2,1:T(2,128)(2,1)S(1)} fusion(bf16[32,3,128,1024]{3,2,1,0:T(8,128)(2,1)} %bitcast.98, s32[]{:T(128)S(6)} %sub.139), kind=kOutput, calls=%fused_computation.10 | convolution fusion | flops 25166496 | bytes 25952260 | tf_op jit(solution)/shard_map/wt,tcxyz->wcxyz/dot_general | solution.py:105
  215.4 16.1 %fusion.21 = f32[3,128,1024]{2,1,0:T(8,128)S(1)} fusion(bf16[1,3,128,1024]{3,0,2,1:T(2,128)(2,1)S(1)} %fusion.7), kind=kOutput, calls=%fused_computation.27 | convolution fusion | flops 821035008 | bytes 2359296 | tf_op jit(solution)/shard_map/dot_general | solution.py:64
  231.5 16.1 %fusion.23 = f32[3,128,1024]{2,1,0:T(8,128)S(1)} fusion(bf16[1,3,128,1024]{3,0,2,1:T(2,128)(2,1)S(1)} %fusion.5), kind=kOutput, calls=%fused_computation.28 | convolution fusion | flops 821035008 | bytes 2359296 | tf_op jit(solution)/shard_map/dot_general | solution.py:61
  247.6 16.5 %fusion.42 = bf16[1,1,3,1,128,1024]{5,4,2,3,1,0:T(8,128)(2,1)S(1)} fusion(f32[3,128,1024]{2,1,0:T(8,128)S(1)} %fusion.21, bf16[1,3,128,1024]{3,0,2,1:T(2,128)(2,1)S(1)} %fusion.5), kind=kOutput, calls=%fused_computation.41 | convolution fusion | flops 821821440 | bytes 3145728 | tf_op jit(solution)/shard_map/dot_general | solution.py:64
  264.1 16.3 %fusion.39 = bf16[1,1,3,1,128,1024]{5,4,2,3,1,0:T(8,128)(2,1)S(1)} fusion(f32[3,128,1024]{2,1,0:T(8,128)S(1)} %fusion.23, bf16[1,3,128,1024]{3,0,2,1:T(2,128)(2,1)S(1)} %fusion.7), kind=kOutput, calls=%fused_computation.40 | convolution fusion | flops 821821440 | bytes 3145728 | tf_op jit(solution)/shard_map/dot_general | solution.py:61
  280.4 0.1 pad_maximum_fusion
  280.6 3.0 copy.44
  283.6 6.7 %all-to-all-start = ((bf16[2,1,3,1,128,1024]{4,0,3,2,1,5:T(2,128)(2,1)}), bf16[2,1,3,1,128,1024]{4,0,3,2,1,5:T(2,128)(2,1)S(1)}, u32[]{:S(2)}, u32[]{:S(2)}) async-start(bf16[2,1,3,1,128,1024]{4,0,3,2,1,5:T(2,128)(2,1)} %copy.44), calls=%async_computation | async-start | bytes 3145728 | tf_op jit(solution)/shard_map/all_to_all | solution.py:111
  290.4 22.9 %all-to-all-done = bf16[2,1,3,1,128,1024]{4,0,3,2,1,5:T(2,128)(2,1)S(1)} async-done(((bf16[2,1,3,1,128,1024]{4,0,3,2,1,5:T(2,128)(2,1)}), bf16[2,1,3,1,128,1024]{4,0,3,2,1,5:T(2,128)(2,1)S(1)}, u32[]{:S(2)}, u32[]{:S(2)}) %all-to-all-start) | async-done | bytes 1572896 | tf_op jit(solution)/shard_map/all_to_all | solution.py:111
  313.3 2.4 copy.45
  315.8 17.9 %fusion.29 = f32[1024,3,128]{2,0,1:T(8,128)S(1)} fusion(bf16[3,1024,128]{2,1,0:T(8,128)(2,1)S(1)} %bitcast.104), kind=kOutput, calls=%fused_computation.31 | convolution fusion | flops 821035008 | bytes 2359296 | tf_op jit(solution)/shard_map/wcxyk,yq->wcxqk/dot_general | solution.py:123
  333.7 18.0 %fusion.19 = f32[1024,3,128]{2,0,1:T(8,128)S(1)} fusion(bf16[3,1024,128]{2,1,0:T(8,128)(2,1)S(1)} %bitcast.105), kind=kOutput, calls=%fused_computation.26 | convolution fusion | flops 821035008 | bytes 2359296 | tf_op jit(solution)/shard_map/wcxyk,yq->wcxqk/dot_general | solution.py:122
  351.6 18.0 %fusion.17 = f32[1024,3,128]{2,0,1:T(8,128)S(1)} fusion(bf16[3,1024,128]{2,1,0:T(8,128)(2,1)S(1)} %bitcast.102), kind=kOutput, calls=%fused_computation.25 | convolution fusion | flops 821035008 | bytes 2359296 | tf_op jit(solution)/shard_map/wcxyk,yq->wcxqk/dot_general | solution.py:125
  369.6 18.0 %add_reduce_fusion = f32[1024,128]{1,0:T(8,128)S(1)} fusion(f32[1024,3,128]{2,0,1:T(8,128)S(1)} %fusion.29, f32[1024,3,128]{2,0,1:T(8,128)S(1)} %fusion.17, f32[1024,3,128]{2,0,1:T(8,128)S(1)} %fusion.19, bf16[3,1024,128]{2,1,0:T(8,128)(2,1)S(1)} %bitcast.103), kind=kOutput, calls=%fused_computation.36 | convolution fusion | flops 823263232 | bytes 6029312 | tf_op jit(solution)/shard_map/wcxyk,yq->wcxqk/dot_general | solution.py:120
  387.7 41.5 %while.14 = (s32[]{:T(128)}, f32[1,128]{1,0:T(1,128)S(1)}, f32[1,1024,128]{2,1,0:T(8,128)S(1)}, s32[1024,128]{1,0:T(8,128)}, s32[]{:T(128)}, /*index=5*/s32[]{:T(128)}, s32[]{:T(128)}, s32[]{:T(128)}) while((s32[]{:T(128)}, f32[1,128]{1,0:T(1,128)S(1)}, f32[1,1024,128]{2,1,0:T(8,128)S(1)}, s32[1024,128]{1,0:T(8,128)}, s32[]{:T(128)}, ...), condition=%wide.region_2.3_spmd.clone, body=%wide.region_1.2_spmd.clone.sunk | while | flops 13631751 | bytes 197789 | solution.py:144
  387.7 0.8 dynamic-slice_bitcast_fusion.2
  388.5 1.8 fusion.113
  390.3 0.8 dynamic-slice_bitcast_fusion.2
  391.1 1.8 fusion.113
  392.9 0.8 dynamic-slice_bitcast_fusion.2
  393.7 1.8 fusion.113
  395.5 0.8 dynamic-slice_bitcast_fusion.2
  396.3 1.8 fusion.113
  398.1 0.8 dynamic-slice_bitcast_fusion.2
  398.9 1.8 fusion.113
  400.7 0.8 dynamic-slice_bitcast_fusion.2
  401.5 1.8 fusion.113
  403.3 0.8 dynamic-slice_bitcast_fusion.2
  404.1 1.8 fusion.113
  405.9 0.8 dynamic-slice_bitcast_fusion.2
  406.6 1.8 fusion.113
  408.5 0.8 dynamic-slice_bitcast_fusion.2
  409.2 1.8 fusion.113
  411.1 0.8 dynamic-slice_bitcast_fusion.2
  411.8 1.8 fusion.113
  413.6 0.8 dynamic-slice_bitcast_fusion.2
  414.4 1.8 fusion.113
  416.2 0.8 dynamic-slice_bitcast_fusion.2
  417.0 1.8 fusion.113
  418.8 0.8 dynamic-slice_bitcast_fusion.2
  419.6 1.8 fusion.113
  421.4 0.8 dynamic-slice_bitcast_fusion.2
  422.2 1.8 fusion.113
  424.0 0.8 dynamic-slice_bitcast_fusion.2
  424.8 1.8 fusion.113
  426.6 0.8 dynamic-slice_bitcast_fusion.2
  427.4 1.8 fusion.113
  429.3 75.6 %psum.7 = f32[8,128]{1,0:T(8,128)S(1)} all-reduce(f32[8,128]{1,0:T(8,128)S(1)} %broadcast_multiply_fusion), channel_id=1, replica_groups=mesh['tm'=32,'gy'=8] {'tm','gy'}, use_global_device_ids=true, to_apply=%region_3.4 | all-reduce | flops 1024 | bytes 8192 | tf_op jit(solution)/shard_map/psum | solution.py:152
  504.9 0.6 add_log_fusion
  (37 shorter events, 0.6 us)
Async XLA Ops:
  7.2 8.7 %copy-start = (bf16[1,3,3,128,1024]{4,3,2,1,0:T(8,128)(2,1)S(1)}, bf16[1,3,3,128,1024]{4,3,2,1,0:T(8,128)(2,1)}, u32[]{:S(2)}) copy-start(bf16[1,3,3,128,1024]{4,3,2,1,0:T(8,128)(2,1)} %param.6) | copy-start | bytes 7077892
  7.2 158.9 %all-gather.2.cloned.1.call-start = ((), (), s32[]{:S(2)}) async-start(), calls=%async_computation.1 | async-start | bytes 25952256 | tf_op jit(solution)/shard_map/all_gather | solution.py:100
  8.5 8.2 %collective-permute-start = (bf16[1,2,1,1,1024]{4,3,2,1,0:T(2,128)(2,1)S(1)}, bf16[1,2,1,1,1024]{4,3,2,1,0:T(2,128)(2,1)S(1)}, u32[]{:S(2)}, u32[]{:S(2)}) collective-permute-start(bf16[1,2,1,1,1024]{4,3,2,1,0:T(2,128)(2,1)S(1)} %get-tuple-element.139), channel_id=1, source_target_pairs={{1,0},{2,1},{3,2},{4,3},{5,4},{6,5},{7,6},{0,7},{9,8},{10,9},{11,1... | collective-permute-start | bytes 12296 | tf_op jit(solution)/shard_map/ppermute | solution.py:23
  14.5 2.0 copy-start.2
  14.5 6.1 %collective-permute-start.1 = (bf16[1,2,1,1,1024]{4,3,2,1,0:T(2,128)(2,1)S(1)}, bf16[1,2,1,1,1024]{4,3,2,1,0:T(2,128)(2,1)S(1)}, u32[]{:S(2)}, u32[]{:S(2)}) collective-permute-start(bf16[1,2,1,1,1024]{4,3,2,1,0:T(2,128)(2,1)S(1)} %get-tuple-element.140), channel_id=1, source_target_pairs={{0,1},{1,2},{2,3},{3,4},{4,5},{5,6},{6,7},{7,0},{8,9},{9,10},{10,1... | collective-permute-start | bytes 12296 | tf_op jit(solution)/shard_map/ppermute | solution.py:21
  280.4 9.9 %copy-start.3 = (s32[9]{0:T(128)S(1)}, s32[9]{0:T(128)}, u32[]{:S(2)}) copy-start(s32[9]{0:T(128)} %param.9) | copy-start | bytes 112
  283.6 29.7 %all-to-all-start = ((bf16[2,1,3,1,128,1024]{4,0,3,2,1,5:T(2,128)(2,1)}), bf16[2,1,3,1,128,1024]{4,0,3,2,1,5:T(2,128)(2,1)S(1)}, u32[]{:S(2)}, u32[]{:S(2)}) async-start(bf16[2,1,3,1,128,1024]{4,0,3,2,1,5:T(2,128)(2,1)} %copy.44), calls=%async_computation | async-start | bytes 3145728 | tf_op jit(solution)/shard_map/all_to_all | solution.py:111
  429.2 76.3 %copy-start.1 = (f32[1,1024,128]{2,1,0:T(8,128)}, f32[1,1024,128]{2,1,0:T(8,128)S(1)}, u32[]{:S(2)}) copy-start(f32[1,1024,128]{2,1,0:T(8,128)S(1)} %get-tuple-element.195) | copy-start | bytes 1572868
Sparse Core Ops, SparseCore 0:
  23.8 142.1 all-gather.1
where the time goes:
time: 518 us; the launch traced here: 513 us
  matrix products  215 us (42%)
  waiting for transfers between devices  169 us (33%)
  blocking collectives  75.6 us (15%)
  local copies, waits for them, and re-layouts  19.7 us (4%)
  between operations  14.5 us (3%)
  starting transfers between devices  12.7 us (2%)
  other arithmetic  5.55 us (1%)
    all_gather x1, waiting for transfers between devices, body(): time_segment = lax.all_gather(electric, 'tm', axis=0, tiled=True)  142 us
    psum x1, blocking collectives, body(): binned = lax.psum(partial_value, ('tm', 'gy'))  75.6 us
    dot_general x16, matrix products, add_block(): return summed + jnp.dot(row_block, onehot, precision=highest)  28.7 us
    dot_general x1, matrix products, body(): jnp.einsum('wt,tcxyz->wcxyz', coefficient_real, time_segment, preferred_e...  24.9 us
    dot_general x1, matrix products, body(): jnp.einsum('wt,tcxyz->wcxyz', coefficient_imaginary, time_segment, prefer...  24.4 us
    all_to_all x1, waiting for transfers between devices, body(): lax.all_to_all(z_turn(re_part.astype(jnp.bfloat16), im_part.astype(jnp.bf...  22.9 us
    dot_general x1, matrix products, body(): jnp.einsum('wcxyk,yq->wcxqk', moved[0], ycos_tab, preferred_element_type=...  18 us
    dot_general x1, matrix products, body(): jnp.einsum('wcxyk,yq->wcxqk', moved[1], ysin_tab, preferred_element_type=...  18 us
  transfers between devices with their start and end apart: 4, of which 3 were waited for; matrix products, arithmetic and copies ran while one was open for 0% of the time, Pallas kernels for 0%

commit v1 on v0

--- a/solution.py
+++ b/solution.py
@@ -97,7 +97,9 @@
     half_count = every_time_sample // 2
     owner_rank = lax.axis_index("tm")
     angular_frequency = owner_rank * local_t + jnp.arange(local_t, dtype=jnp.int32) - half_count
-    time_segment = lax.all_gather(electric, "tm", axis=0, tiled=True)
+    time_segment = jnp.concatenate(
+        lax.all_to_all(jnp.stack([electric] * lax.axis_size("tm")), "tm", 0, 0), axis=0
+    )
     sample_moments = jnp.arange(time_segment.shape[0], dtype=jnp.int32)
     coefficient_real, coefficient_imaginary = temporal_coefficients(
         angular_frequency, sample_moments, every_time_sample

time: 518 us -> 939 us (1.81)
  waiting for transfers between devices: 169 us -> 561 us
  blocking collectives: 75.6 us -> 102 us
  between operations: 14.5 us -> 1.1 us
    all_to_all x0 -> x1, waiting for transfers between devices: none -> 543 us  [body(): lax.all_to_all(jnp.stack([electric] * lax.axis_size('tm')), 'tm', 0, 0)]
    all_gather x1 -> x0, waiting for transfers between devices: 142 us -> none  [body(): time_segment = lax.all_gather(electric, 'tm', axis=0, tiled=True)]
    psum x1, blocking collectives: 75.6 us -> 102 us  [body(): binned = lax.psum(partial_value, ('tm', 'gy'))]
    all_to_all x0 -> x1, starting transfers between devices: none -> 11.2 us  [body(): lax.all_to_all(jnp.stack([electric] * lax.axis_size('tm')), 'tm', 0, 0)]
where the time goes in v1:
time: 939 us; the launch traced here: 934 us
  waiting for transfers between devices  561 us (60%)
  matrix products  215 us (23%)
  blocking collectives  102 us (11%)
  local copies, waits for them, and re-layouts  28.5 us (3%)
  starting transfers between devices  21 us (2%)
    all_to_all x1, waiting for transfers between devices, body(): lax.all_to_all(jnp.stack([electric] * lax.axis_size('tm')), 'tm', 0, 0)  543 us
    psum x1, blocking collectives, body(): binned = lax.psum(partial_value, ('tm', 'gy'))  102 us
    dot_general x16, matrix products, add_block(): return summed + jnp.dot(row_block, onehot, precision=highest)  28.7 us
    dot_general x1, matrix products, body(): jnp.einsum('wt,tcxyz->wcxyz', coefficient_real, time_segment, preferred_e...  24.9 us
    dot_general x1, matrix products, body(): jnp.einsum('wt,tcxyz->wcxyz', coefficient_imaginary, time_segment, prefer...  24.3 us
  transfers between devices with their start and end apart: 4, of which 3 were waited for; matrix products, arithmetic and copies ran while one was open for 0% of the time, Pallas kernels for 0%

profile of v1, /device:TPU:1, one launch (start us, length us, event | category | flops | bytes accessed | tf_op | source)
XLA Modules:
  0.0 934.0 jit_solution(10483097301150634521)
XLA Ops:
  0.6 1.2 fusion.106
  1.9 6.0 collective-permute-start
  7.9 1.4 slice_convert_fusion
  9.3 0.3 subtract_multiply_fusion
  9.6 0.2 slice_bitcast_fusion.1
  9.9 0.2 convert_element_type.196
  10.1 3.9 collective-permute-done.1
  14.0 0.3 subtract_multiply_fusion.1
  14.3 0.6 fusion.48
  14.8 0.2 slice_bitcast_fusion.3
  15.1 0.6 fusion.47
  15.7 0.3 fusion.49
  16.1 8.7 stack.23
  24.9 11.2 %all-to-all-start = ((bf16[32,1,3,1,128,1024]{5,4,3,2,1,0:T(8,128)(2,1)}), bf16[32,1,3,1,128,1024]{5,4,3,2,1,0:T(8,128)(2,1)}, u32[]{:S(2)}, u32[]{:S(2)}) async-start(bf16[32,1,3,1,128,1024]{5,4,3,2,1,0:T(8,128)(2,1)} %stack.23), calls=%async_computation | async-start | bytes 50331648 | tf_op jit(solution)/shard_map/all_to_all | solution.py:101
  36.1 542.8 %all-to-all-done = bf16[32,1,3,1,128,1024]{5,4,3,2,1,0:T(8,128)(2,1)} async-done(((bf16[32,1,3,1,128,1024]{5,4,3,2,1,0:T(8,128)(2,1)}), bf16[32,1,3,1,128,1024]{5,4,3,2,1,0:T(8,128)(2,1)}, u32[]{:S(2)}, u32[]{:S(2)}) %all-to-all-start) | async-done | bytes 25165856 | tf_op jit(solution)/shard_map/all_to_all | solution.py:101
  578.9 24.3 %fusion.5 = bf16[1,3,128,1024]{3,0,2,1:T(2,128)(2,1)S(1)} fusion(bf16[32,3,128,1024]{3,2,1,0:T(8,128)(2,1)} %bitcast.17, s32[]{:T(128)S(6)} %sub.139), kind=kOutput, calls=%fused_computation.8 | convolution fusion | flops 25166528 | bytes 25952260 | tf_op jit(solution)/shard_map/wt,tcxyz->wcxyz/dot_general | solution.py:110
  603.2 24.9 %fusion.7 = bf16[1,3,128,1024]{3,0,2,1:T(2,128)(2,1)S(1)} fusion(bf16[32,3,128,1024]{3,2,1,0:T(8,128)(2,1)} %bitcast.17, s32[]{:T(128)S(6)} %sub.139), kind=kOutput, calls=%fused_computation.10 | convolution fusion | flops 25166496 | bytes 25952260 | tf_op jit(solution)/shard_map/wt,tcxyz->wcxyz/dot_general | solution.py:107
  628.1 16.1 %fusion.23 = f32[3,128,1024]{2,1,0:T(8,128)S(1)} fusion(bf16[1,3,128,1024]{3,0,2,1:T(2,128)(2,1)S(1)} %fusion.5), kind=kOutput, calls=%fused_computation.28 | convolution fusion | flops 821035008 | bytes 2359296 | tf_op jit(solution)/shard_map/dot_general | solution.py:61
  644.2 16.1 %fusion.21 = f32[3,128,1024]{2,1,0:T(8,128)S(1)} fusion(bf16[1,3,128,1024]{3,0,2,1:T(2,128)(2,1)S(1)} %fusion.7), kind=kOutput, calls=%fused_computation.27 | convolution fusion | flops 821035008 | bytes 2359296 | tf_op jit(solution)/shard_map/dot_general | solution.py:64
  660.3 16.5 %fusion.39 = bf16[1,1,3,1,128,1024]{5,4,2,3,1,0:T(8,128)(2,1)S(1)} fusion(f32[3,128,1024]{2,1,0:T(8,128)S(1)} %fusion.23, bf16[1,3,128,1024]{3,0,2,1:T(2,128)(2,1)S(1)} %fusion.7), kind=kOutput, calls=%fused_computation.40 | convolution fusion | flops 821821440 | bytes 3145728 | tf_op jit(solution)/shard_map/dot_general | solution.py:61
  676.8 16.3 %fusion.42 = bf16[1,1,3,1,128,1024]{5,4,2,3,1,0:T(8,128)(2,1)S(1)} fusion(f32[3,128,1024]{2,1,0:T(8,128)S(1)} %fusion.21, bf16[1,3,128,1024]{3,0,2,1:T(2,128)(2,1)S(1)} %fusion.5), kind=kOutput, calls=%fused_computation.41 | convolution fusion | flops 821821440 | bytes 3145728 | tf_op jit(solution)/shard_map/dot_general | solution.py:64
  693.3 3.0 copy.44
  696.3 3.8 all-to-all-start.1
  700.2 14.5 %all-to-all-done.1 = bf16[2,1,3,1,128,1024]{4,0,3,2,1,5:T(2,128)(2,1)S(1)} async-done(((bf16[2,1,3,1,128,1024]{4,0,3,2,1,5:T(2,128)(2,1)}), bf16[2,1,3,1,128,1024]{4,0,3,2,1,5:T(2,128)(2,1)S(1)}, u32[]{:S(2)}, u32[]{:S(2)}) %all-to-all-start.1) | async-done | bytes 1572896 | tf_op jit(solution)/shard_map/all_to_all | solution.py:113
  714.7 2.4 copy.45
  717.2 18.0 %fusion.19 = f32[1024,3,128]{2,0,1:T(8,128)S(1)} fusion(bf16[3,1024,128]{2,1,0:T(8,128)(2,1)S(1)} %bitcast.108), kind=kOutput, calls=%fused_computation.26 | convolution fusion | flops 821035008 | bytes 2359296 | tf_op jit(solution)/shard_map/wcxyk,yq->wcxqk/dot_general | solution.py:124
  735.2 17.9 %fusion.29 = f32[1024,3,128]{2,0,1:T(8,128)S(1)} fusion(bf16[3,1024,128]{2,1,0:T(8,128)(2,1)S(1)} %bitcast.109), kind=kOutput, calls=%fused_computation.31 | convolution fusion | flops 821035008 | bytes 2359296 | tf_op jit(solution)/shard_map/wcxyk,yq->wcxqk/dot_general | solution.py:125
  753.1 18.0 %fusion.17 = f32[1024,3,128]{2,0,1:T(8,128)S(1)} fusion(bf16[3,1024,128]{2,1,0:T(8,128)(2,1)S(1)} %bitcast.106), kind=kOutput, calls=%fused_computation.25 | convolution fusion | flops 821035008 | bytes 2359296 | tf_op jit(solution)/shard_map/wcxyk,yq->wcxqk/dot_general | solution.py:127
  771.0 18.1 %add_reduce_fusion = f32[1024,128]{1,0:T(8,128)S(1)} fusion(f32[1024,3,128]{2,0,1:T(8,128)S(1)} %fusion.29, f32[1024,3,128]{2,0,1:T(8,128)S(1)} %fusion.17, f32[1024,3,128]{2,0,1:T(8,128)S(1)} %fusion.19, bf16[3,1024,128]{2,1,0:T(8,128)(2,1)S(1)} %bitcast.107), kind=kOutput, calls=%fused_computation.36 | convolution fusion | flops 823263232 | bytes 6029312 | tf_op jit(solution)/shard_map/wcxyk,yq->wcxqk/dot_general | solution.py:122
  789.2 41.7 %while.14 = (s32[]{:T(128)}, f32[1,128]{1,0:T(1,128)S(1)}, f32[1,1024,128]{2,1,0:T(8,128)S(1)}, s32[1024,128]{1,0:T(8,128)}, s32[]{:T(128)}, /*index=5*/s32[]{:T(128)}, s32[]{:T(128)}, s32[]{:T(128)}) while((s32[]{:T(128)}, f32[1,128]{1,0:T(1,128)S(1)}, f32[1,1024,128]{2,1,0:T(8,128)S(1)}, s32[1024,128]{1,0:T(8,128)}, s32[]{:T(128)}, ...), condition=%wide.region_2.3_spmd.clone, body=%wide.region_1.2_spmd.clone.sunk | while | flops 13631751 | bytes 197781 | solution.py:146
  789.2 0.8 dynamic-slice_bitcast_fusion.2
  790.0 1.8 fusion.116
  791.8 0.8 dynamic-slice_bitcast_fusion.2
  792.6 1.8 fusion.116
  794.4 0.8 dynamic-slice_bitcast_fusion.2
  795.2 1.8 fusion.116
  797.0 0.8 dynamic-slice_bitcast_fusion.2
  797.8 1.8 fusion.116
  799.6 0.8 dynamic-slice_bitcast_fusion.2
  800.4 1.8 fusion.116
  802.2 0.8 dynamic-slice_bitcast_fusion.2
  803.0 1.8 fusion.116
  804.8 0.8 dynamic-slice_bitcast_fusion.2
  805.6 1.8 fusion.116
  807.4 0.8 dynamic-slice_bitcast_fusion.2
  808.2 1.8 fusion.116
  810.0 0.8 dynamic-slice_bitcast_fusion.2
  810.8 1.8 fusion.116
  812.6 0.8 dynamic-slice_bitcast_fusion.2
  813.4 1.8 fusion.116
  815.2 0.8 dynamic-slice_bitcast_fusion.2
  816.0 1.8 fusion.116
  817.8 0.8 dynamic-slice_bitcast_fusion.2
  818.6 1.8 fusion.116
  820.5 0.8 dynamic-slice_bitcast_fusion.2
  821.2 1.8 fusion.116
  823.1 0.8 dynamic-slice_bitcast_fusion.2
  823.8 1.8 fusion.116
  825.7 0.8 dynamic-slice_bitcast_fusion.2
  826.4 1.8 fusion.116
  828.3 0.8 dynamic-slice_bitcast_fusion.2
  829.0 1.8 fusion.116
  830.9 102.2 %psum.7 = f32[8,128]{1,0:T(8,128)S(1)} all-reduce(f32[8,128]{1,0:T(8,128)S(1)} %broadcast_multiply_fusion), channel_id=1, replica_groups=mesh['tm'=32,'gy'=8] {'tm','gy'}, use_global_device_ids=true, to_apply=%region_3.4 | all-reduce | flops 1024 | bytes 8192 | tf_op jit(solution)/shard_map/psum | solution.py:154
  933.2 0.6 add_log_fusion
  (37 shorter events, 0.9 us)
Async XLA Ops:
  0.6 8.7 copy-start
  1.9 8.2 collective-permute-start
  7.9 2.0 copy-start.2
  7.9 6.1 collective-permute-start.1
  24.9 554.0 %all-to-all-start = ((bf16[32,1,3,1,128,1024]{5,4,3,2,1,0:T(8,128)(2,1)}), bf16[32,1,3,1,128,1024]{5,4,3,2,1,0:T(8,128)(2,1)}, u32[]{:S(2)}, u32[]{:S(2)}) async-start(bf16[32,1,3,1,128,1024]{5,4,3,2,1,0:T(8,128)(2,1)} %stack.23), calls=%async_computation | async-start | bytes 50331648 | tf_op jit(solution)/shard_map/all_to_all | solution.py:101
  693.1 7.0 copy-start.3
  696.3 18.4 %all-to-all-start.1 = ((bf16[2,1,3,1,128,1024]{4,0,3,2,1,5:T(2,128)(2,1)}), bf16[2,1,3,1,128,1024]{4,0,3,2,1,5:T(2,128)(2,1)S(1)}, u32[]{:S(2)}, u32[]{:S(2)}) async-start(bf16[2,1,3,1,128,1024]{4,0,3,2,1,5:T(2,128)(2,1)} %copy.44), calls=%async_computation.1 | async-start | bytes 3145728 | tf_op jit(solution)/shard_map/all_to_all | solution.py:113
  830.8 102.9 %copy-start.1 = (f32[1,1024,128]{2,1,0:T(8,128)}, f32[1,1024,128]{2,1,0:T(8,128)S(1)}, u32[]{:S(2)}) copy-start(f32[1,1024,128]{2,1,0:T(8,128)S(1)} %get-tuple-element.193) | copy-start | bytes 1572868
